TPU v7x, 128 devices: a whole 4x4x4 slice. The times are simulated.
128 devices in a mesh: dp: 16 (over x_lo, z, core), seq: 8 (over x_hi, y).
Axes of the slice: x: 4 (x_hi: 2, x_lo: 2; x = x_hi * 2 + x_lo), y: 4, z: 4, core: 2. Of those that a mesh axis runs over, the one named last changes fastest.
Arguments:
- video: bfloat16 [16, 8, 256, 1152], P('dp', 'seq'), may hold values from -6 to 6
- out_grad: bfloat16 [16, 8, 256, 1152], P('dp', 'seq'), may hold values from -6 to 6
- gain_spatial: float32 [1152], replicated, may hold values from 0.1 to 1.9
- gain_temporal: float32 [1152], replicated, may hold values from 0.1 to 1.9
- w_spatial_qkv: bfloat16 [1152, 3456], replicated, may hold values from -4 to 4
- w_spatial_out: bfloat16 [1152, 1152], replicated, may hold values from -0.1875 to 0.1875
- w_temporal_qkv: bfloat16 [1152, 3456], replicated, may hold values from -4 to 4
- w_temporal_out: bfloat16 [1152, 1152], replicated, may hold values from -0.1875 to 0.1875
Outputs:
- video_grad: bfloat16 [16, 8, 256, 1152], P('dp', 'seq')
- w_grad: float32 [1152, 1152], P(('dp', 'seq'))
All inputs are finite; a program needn't handle non-finite values.
Results may differ from a plain program's by a relative error of at most 0.018.
Values may be sent and summed in bfloat16 or wider, within the bound.
No kernel may reach another device: no remote copies, remote signals or barrier semaphores. Data moves between devices by JAX's collectives and lax.ppermute only.
A program may use at most 128 MiB of HBM per device.

v0:
```python
import math
import jax
import jax.numpy as jnp
from jax import lax
from jax.sharding import PartitionSpec as P

HEADS = 16
epsilon = 1e-06


def layer_norm(stream, gain_vec):
    center = jnp.mean(stream, axis=-1, keepdims=True)
    centered = stream - center
    spread = jnp.mean(centered * centered, axis=-1, keepdims=True)
    return (centered * lax.rsqrt(spread + epsilon) * gain_vec).astype(jnp.bfloat16)


def project(hidden, weight):
    return jnp.dot(hidden, weight, preferred_element_type=jnp.float32)


def split_heads(block):
    shape = block.shape[:-1] + (HEADS, block.shape[-1] // HEADS)
    return block.reshape(shape).astype(jnp.float32)


def spatial_mix(qkv):
    width = qkv.shape[-1] // 3
    query_part = split_heads(qkv[..., :width])
    key_part = split_heads(qkv[..., width : 2 * width])
    value_part = split_heads(qkv[..., 2 * width :])
    scale = 1.0 / math.sqrt(width // HEADS)
    scores = (
        jnp.einsum("bfqhd,bfkhd->bfhqk", query_part, key_part, precision=lax.Precision.HIGHEST)
        * scale
    )
    weights = jax.nn.softmax(scores, axis=-1)
    mixed = jnp.einsum("bfhqk,bfkhd->bfqhd", weights, value_part, precision=lax.Precision.HIGHEST)
    return mixed.reshape(qkv.shape[:-1] + (width,)).astype(jnp.bfloat16)


def temporal_mix(qkv):
    width = qkv.shape[-1] // 3
    query_part = split_heads(qkv[..., :width])
    key_part = split_heads(qkv[..., width : 2 * width])
    value_part = split_heads(qkv[..., 2 * width :])
    scale = 1.0 / math.sqrt(width // HEADS)
    scores = (
        jnp.einsum("bqphd,bkphd->bphqk", query_part, key_part, precision=lax.Precision.HIGHEST)
        * scale
    )
    weights = jax.nn.softmax(scores, axis=-1)
    mixed = jnp.einsum("bphqk,bkphd->bqphd", weights, value_part, precision=lax.Precision.HIGHEST)
    return mixed.reshape(qkv.shape[:-1] + (width,)).astype(jnp.bfloat16)


def spatial_section(clip, gain_vec, w_qkv, w_out):
    hidden = layer_norm(clip.astype(jnp.float32), gain_vec)
    qkv = project(hidden, w_qkv).astype(jnp.bfloat16)
    return clip.astype(jnp.float32) + project(spatial_mix(qkv), w_out)


def token_outer(mixed, grad_rows):
    width = mixed.shape[-1]
    return lax.dot_general(
        mixed.reshape(-1, width),
        grad_rows.reshape(-1, width),
        (((0,), (0,)), ((), ())),
        preferred_element_type=jnp.float32,
    )


def per_device(
    video,
    out_grad,
    gain_spatial,
    gain_temporal,
    w_spatial_qkv,
    w_spatial_out,
    w_temporal_qkv,
    w_temporal_out,
):
    token_total = (
        lax.axis_size("dp")
        * lax.axis_size("seq")
        * video.shape[0]
        * video.shape[1]
        * video.shape[2]
    )
    stream, spatial_back = jax.vjp(
        lambda clip_in: spatial_section(clip_in, gain_spatial, w_spatial_qkv, w_spatial_out), video
    )
    grad_float = out_grad.astype(jnp.float32)
    qkv, pre_back = jax.vjp(
        lambda stream_in: project(layer_norm(stream_in, gain_temporal), w_temporal_qkv).astype(
            jnp.bfloat16
        ),
        stream,
    )
    moved_qkv = lax.all_to_all(qkv, "seq", split_axis=2, concat_axis=1, tiled=True)
    mixed_pos, mix_back = jax.vjp(temporal_mix, moved_qkv)
    mixed = lax.all_to_all(mixed_pos, "seq", split_axis=1, concat_axis=2, tiled=True)
    local_sum = token_outer(mixed, out_grad)
    unused, out_back = jax.vjp(lambda mixed_in: project(mixed_in, w_temporal_out), mixed)
    mixed_grad = out_back(grad_float)[0]
    mixed_grad_pos = lax.all_to_all(mixed_grad, "seq", split_axis=2, concat_axis=1, tiled=True)
    qkv_grad_pos = mix_back(mixed_grad_pos)[0]
    qkv_grad = lax.all_to_all(qkv_grad_pos, "seq", split_axis=1, concat_axis=2, tiled=True)
    stream_grad = grad_float + pre_back(qkv_grad)[0]
    video_grad = spatial_back(stream_grad)[0]
    local_sum = local_sum / math.sqrt(float(token_total))
    w_grad = lax.psum_scatter(local_sum, ("dp", "seq"), scatter_dimension=0, tiled=True)
    return (video_grad, w_grad)


def solution(mesh):
    return jax.shard_map(
        per_device,
        mesh=mesh,
        in_specs=(
            P("dp", "seq", None, None),
            P("dp", "seq", None, None),
            P(),
            P(),
            P(),
            P(),
            P(),
            P(),
        ),
        out_specs=(P("dp", "seq", None, None), P(("dp", "seq"), None)),
        check_vma=False,
    )
```

profile of v0, /device:TPU:1, one launch (start us, length us, event | category | flops | bytes accessed | tf_op | source)
XLA Modules:
  0.0 361.7 jit_solution(15675530483380894013)
XLA Ops:
  7.2 3.1 fusion.7
  12.8 6.0 %reduce.23 = bf16[256,1152]{1,0:T(8,128)(2,1)} reduce(bf16[256,1,1,1152]{3,2,1,0:T(2,128)(2,1)} %bitcast.153, bf16[]{:T(256)} %broadcast.212), dimensions={1,2}, to_apply=%bitcast.145.reduce_sub_computation | reduce | bytes 1179650
  18.9 2.6 reshape.406
  21.4 7.7 %all-to-all-start = ((bf16[8,2,18432]{2,1,0:T(2,128)(2,1)}), bf16[8,2,18432]{2,1,0:T(2,128)(2,1)}, u32[]{:S(2)}, u32[]{:S(2)}) async-start(bf16[8,2,18432]{2,1,0:T(2,128)(2,1)} %reshape.406), calls=%async_computation | async-start | bytes 1179648 | tf_op jit(solution)/shard_map/all_to_all | solution.py:106
  29.7 5.9 %fusion = bf16[1,1,256,3456]{3,2,1,0:T(8,128)(2,1)S(1)} fusion(bf16[1152,3456]{1,0:T(8,128)(2,1)} %param.12, bf16[1,1,256,1152]{3,2,1,0:T(8,128)(2,1)S(1)} %copy-done.4, f32[1152]{0:T(1024)S(1)} %copy-done.26, f32[256]{0:T(256)S(1)} %fusion.57, f32[256]{0:T(256)S(1)} %broadcast_multiply_fusion.1), kind=kOutput, calls=%fused_computation.3 | convolution fusion | flops 2040791040 | bytes 10328576 | tf_op jit(solution)/shard_map/jvp()/dot_general | solution.py:19
  36.9 2.1 copy.73
  39.0 2.1 copy.72
  41.1 2.1 copy.71
  43.2 2.0 multiply_reduce_fusion.1
  47.4 2.4 convolution_convert_fusion.13
  52.0 2.7 fusion.1
  54.7 5.0 %copy.131 = bf16[1,1,256,3456]{3,1,0,2:T(2,128)(2,1)} copy(bf16[1,1,256,3456]{3,2,1,0:T(8,128)(2,1)S(1)} %fusion.1) | data formatting | bytes 3538944 | tf_op jit(solution)/shard_map/jvp()/convert_element_type | solution.py:95
  59.7 13.1 %reduce.22 = bf16[256,3456]{1,0:T(8,128)(2,1)} reduce(bf16[256,1,1,3456]{3,2,1,0:T(2,128)(2,1)} %bitcast.146, bf16[]{:T(256)} %broadcast.212), dimensions={1,2}, to_apply=%bitcast.144.reduce_sub_computation | reduce | bytes 3538946
  72.8 5.7 %reshape.404 = bf16[8,2,55296]{2,1,0:T(2,128)(2,1)} reshape(bf16[256,3456]{1,0:T(8,128)(2,1)} %reduce.22) | data formatting | bytes 3538944
  78.5 6.6 %all-to-all-start.1 = ((bf16[8,2,55296]{2,1,0:T(2,128)(2,1)}), bf16[8,2,55296]{2,1,0:T(2,128)(2,1)}, u32[]{:S(2)}, u32[]{:S(2)}) async-start(bf16[8,2,55296]{2,1,0:T(2,128)(2,1)} %reshape.404), calls=%async_computation.1 | async-start | bytes 3538944 | tf_op jit(solution)/shard_map/all_to_all | solution.py:100
  85.2 3.5 reshape.407
  88.7 5.5 %bitcast_reduce_fusion = bf16[256,1152]{1,0:T(8,128)(2,1)} fusion(bf16[256,1,1,1152]{3,2,1,0:T(2,128)(2,1)} %reshape.407), kind=kLoop, calls=%fused_computation.115 | loop fusion | bytes 1179648 | tf_op jit(solution)/shard_map/all_to_all | solution.py:106
  94.2 3.7 %reshape.381 = bf16[1,8,32,16,72]{4,3,2,1,0:T(8,128)(2,1)} reshape(bf16[256,1152]{1,0:T(8,128)(2,1)} %bitcast_reduce_fusion) | data formatting | bytes 1179648 | tf_op jit(solution)/shard_map/transpose(jvp())/reshape | solution.py:54
  97.9 9.9 %all-to-all-done.1 = bf16[8,2,55296]{2,1,0:T(2,128)(2,1)} async-done(((bf16[8,2,55296]{2,1,0:T(2,128)(2,1)}), bf16[8,2,55296]{2,1,0:T(2,128)(2,1)}, u32[]{:S(2)}, u32[]{:S(2)}) %all-to-all-start.1) | async-done | bytes 1769504 | tf_op jit(solution)/shard_map/all_to_all | solution.py:100
  107.9 6.5 %reshape.405 = bf16[256,1,1,3456]{3,2,1,0:T(2,128)(2,1)} reshape(bf16[8,2,55296]{2,1,0:T(2,128)(2,1)} %all-to-all-done.1) | data formatting | bytes 3538944
  114.4 2.2 copy.100
  117.9 3.7 %reshape.388 = bf16[8,32,16,72]{3,2,1,0:T(8,128)(2,1)} reshape(bf16[1,8,32,1152]{3,2,1,0:T(8,128)(2,1)} %get-tuple-element.4) | data formatting | bytes 1179648 | tf_op jit(solution)/shard_map/reshape.54
  121.6 3.7 %reshape.391 = bf16[8,32,16,72]{3,2,1,0:T(8,128)(2,1)} reshape(bf16[1,8,32,1152]{3,2,1,0:T(8,128)(2,1)} %get-tuple-element.5) | data formatting | bytes 1179648 | tf_op jit(solution)/shard_map/reshape.63
  125.3 3.9 %reshape.389 = bf16[8,32,16,72]{3,2,1,0:T(8,128)(2,1)} reshape(bf16[1,8,32,1152]{3,2,1,0:T(8,128)(2,1)} %get-tuple-element.6) | data formatting | bytes 1179648 | tf_op jit(solution)/shard_map/reshape.55
  129.2 3.2 multiply_reduce_fusion.3
  134.4 2.8 fusion.22
  137.2 2.3 multiply_reduce_fusion.2
  139.6 4.1 %fusion.21 = bf16[1,8,32,16,72]{4,1,3,2,0:T(8,128)(2,1)} fusion(bf16[8,32,16,72]{3,2,1,0:T(8,128)(2,1)S(1)} %copy-done.13, f32[32,16,8,8]{2,3,1,0:T(8,128)S(1)} %get-tuple-element.17, f32[32,16,8]{2,1,0:T(8,128)S(1)} %neg.20, f32[32,16,8]{2,1,0:T(8,128)S(1)} %fusion.56, f32[32,16,8]{2,1,0:T(8,128)S(1)} %get-tuple-element.14, ...), kind=kOutput, calls=%fused_computation.47 | convolution fusion | flops 28803072 | bytes 1490944 | tf_op jit(solution)/shard_map/transpose(jvp(bqphd,bkphd->bphqk))/dot_general | solution.py:49
  143.7 3.8 %fusion.20 = bf16[1,8,32,16,72]{4,1,3,2,0:T(8,128)(2,1)} fusion(bf16[8,32,16,72]{3,2,1,0:T(8,128)(2,1)S(1)} %copy-done.12, f32[32,16,8,8]{2,3,1,0:T(8,128)S(1)} %get-tuple-element.17, f32[32,16,8]{2,1,0:T(8,128)S(1)} %neg.20, f32[32,16,8]{2,1,0:T(8,128)S(1)} %fusion.56, f32[32,16,8]{2,1,0:T(8,128)S(1)} %get-tuple-element.14, ...), kind=kOutput, calls=%fused_computation.46 | convolution fusion | flops 28803072 | bytes 1490944 | tf_op jit(solution)/shard_map/transpose(jvp(bqphd,bkphd->bphqk))/dot_general | solution.py:49
  148.6 2.9 convert_element_type.198
  151.6 5.6 %all-to-all-start.3 = ((bf16[1,8,32,1152]{3,2,0,1:T(8,128)(2,1)}), bf16[1,8,32,1152]{3,2,0,1:T(8,128)(2,1)}, u32[]{:S(2)}, u32[]{:S(2)}) async-start(bf16[1,8,32,1152]{3,2,0,1:T(8,128)(2,1)} %bitcast.158), calls=%async_computation.3 | async-start | bytes 1179648 | tf_op jit(solution)/shard_map/all_to_all | solution.py:102
  157.1 4.6 %fusion.19 = bf16[1,8,32,16,72]{4,1,3,2,0:T(8,128)(2,1)S(1)} fusion(bf16[1,8,32,16,72]{4,3,2,1,0:T(8,128)(2,1)} %reshape.381, f32[32,16,8]{2,1,0:T(8,128)} %copy-done.19, f32[32,16,8,8]{2,3,1,0:T(8,128)} %copy-done.3, f32[32,16,8]{2,1,0:T(8,128)S(1)} %get-tuple-element.14), kind=kOutput, calls=%fused_computation.45 | convolution fusion | flops 28704768 | bytes 1343488 | tf_op jit(solution)/shard_map/transpose(jvp(bphqk,bkphd->bqphd))/dot_general | solution.py:53
  162.9 2.9 reshape.390
  165.8 2.3 copy.81
  168.1 2.9 reshape.392
  171.0 2.3 copy.84
  173.4 2.9 reshape.393
  176.3 2.8 add_bitcast_fusion
  179.1 6.6 %all-to-all-start.2 = ((bf16[1,8,32,3456]{3,2,0,1:T(8,128)(2,1)}), bf16[1,8,32,3456]{3,2,0,1:T(8,128)(2,1)}, u32[]{:S(2)}, u32[]{:S(2)}) async-start(bf16[1,8,32,3456]{3,2,0,1:T(8,128)(2,1)} %add_bitcast_fusion), calls=%async_computation.2 | async-start | bytes 3538944 | tf_op jit(solution)/shard_map/all_to_all | solution.py:108
  186.2 4.6 %convolution_multiply_fusion = f32[1152,1152]{1,0:T(8,128)} fusion(bf16[256,1152]{1,0:T(8,128)(2,1)} %bitcast.47, bf16[1,1,256,1152]{3,2,1,0:T(8,128)(2,1)} %param.9), kind=kOutput, calls=%fused_computation | convolution fusion | flops 680804352 | bytes 6488064 | tf_op jit(solution)/shard_map/dot_general | solution.py:65
  190.8 18.2 %all-to-all-done.2 = bf16[1,8,32,3456]{3,2,0,1:T(8,128)(2,1)} async-done(((bf16[1,8,32,3456]{3,2,0,1:T(8,128)(2,1)}), bf16[1,8,32,3456]{3,2,0,1:T(8,128)(2,1)}, u32[]{:S(2)}, u32[]{:S(2)}) %all-to-all-start.2) | async-done | bytes 1769504 | tf_op jit(solution)/shard_map/all_to_all | solution.py:108
  209.1 6.8 %fusion.28 = (f32[256]{0:T(256)S(1)}, f32[256,1152]{1,0:T(8,128)S(1)}) fusion(f32[1,1,256,1152]{3,2,1,0:T(8,128)} %copy-done.7, f32[256]{0:T(256)S(1)} %copy-done.21, f32[1152]{0:T(1024)S(1)} %copy-done.25, bf16[256,3456]{1,0:T(8,128)(2,1)} %bitcast.23, bf16[1152,3456]{1,0:T(8,128)(2,1)} %param.14), kind=kOutput, calls=%fused_computation.59 | convolution fusion | flops 2040200960 | bytes 12098048 | tf_op jit(solution)/shard_map/transpose(jvp())/dot_general | solution.py:19
  219.2 2.1 copy.86
  221.4 4.1 %multiply_reduce_fusion = (f32[16,256]{1,0:T(8,128)S(1)}, f32[16,256,256]{1,2,0:T(8,128)S(1)}) fusion(f32[16,256]{1,0:T(8,128)S(1)} %multiply_divide_fusion.1, f32[16,256]{1,0:T(8,128)S(1)} %get-tuple-element.10, f32[16,256,256]{1,2,0:T(8,128)} %copy-done.1, bf16[16,72,256]{2,1,0:T(8,128)(2,1)} %bitcast.156, bf16[256,16,72]{0,2,1:T(8,128)(2,1)} %bitcast.154), kind=kOutput, calls=%fused_computation.6 | convolution fusion | flops 156233728 | bytes 9617408 | tf_op jit(solution)/shard_map/transpose(jvp(bfhqk,bfkhd->bfqhd))/dot_general | solution.py:38
  228.5 2.3 convolution_convert_fusion.11
  230.8 3.1 convolution_convert_fusion.12
  233.9 2.8 fusion.26
  239.5 113.6 %all-reduce.9.cloned.1.call-done = f32[1152,1152]{1,0:T(8,128)} async-done(((f32[1152,1152]{1,0:T(8,128)}), f32[1152,1152]{1,0:T(8,128)}) %all-reduce.9.cloned.1.call-update) | async-done | bytes 5308432
  (101 shorter events, 25.3 us)
Async XLA Ops:
  7.2 42.6 %copy-start = (bf16[1152,1152]{1,0:T(8,128)(2,1)S(1)}, bf16[1152,1152]{1,0:T(8,128)(2,1)}, u32[]{:S(2)}) copy-start(bf16[1152,1152]{1,0:T(8,128)(2,1)} %param.13) | copy-start | bytes 7962628
  12.2 17.0 %copy-start.4 = (bf16[1,1,256,1152]{3,2,1,0:T(8,128)(2,1)S(1)}, bf16[1,1,256,1152]{3,2,1,0:T(8,128)(2,1)}, u32[]{:S(2)}) copy-start(bf16[1,1,256,1152]{3,2,1,0:T(8,128)(2,1)} %param.8) | copy-start | bytes 1769476
  18.9 10.8 %copy-start.26 = (f32[1152]{0:T(1024)S(1)}, f32[1152]{0:T(1024)}, u32[]{:S(2)}) copy-start(f32[1152]{0:T(1024)} %param.10) | copy-start | bytes 13828
  21.4 57.1 %all-to-all-start = ((bf16[8,2,18432]{2,1,0:T(2,128)(2,1)}), bf16[8,2,18432]{2,1,0:T(2,128)(2,1)}, u32[]{:S(2)}, u32[]{:S(2)}) async-start(bf16[8,2,18432]{2,1,0:T(2,128)(2,1)} %reshape.406), calls=%async_computation | async-start | bytes 1179648 | tf_op jit(solution)/shard_map/all_to_all | solution.py:106
  45.3 2.1 copy-start.1
  45.3 2.1 copy-start.15
  45.3 6.7 %slice-start = ((s8[7962624]{0:T(1024)(128)(4,1)}), s8[4194304]{0:T(1024)(128)(4,1)S(1)}, s32[]{:S(2)}) async-start(s8[7962624]{0:T(1024)(128)(4,1)} %bitcast.161), calls=%async_computation.5 | async-start | bytes 8388608
  47.4 4.6 %slice-start.1 = ((s8[7962624]{0:T(1024)(128)(4,1)}), s8[3768320]{0:T(1024)(128)(4,1)S(1)}, s32[]{:S(2)}) async-start(s8[7962624]{0:T(1024)(128)(4,1)} %bitcast.161), calls=%async_computation.6 | async-start | bytes 7536640
  49.8 2.2 copy-start.24
  51.0 1.0 copy-start.7
  51.0 3.7 %copy-start.20 = (f32[256]{0:T(256)}, f32[256]{0:T(256)S(1)}, u32[]{:S(2)}) copy-start(f32[256]{0:T(256)S(1)} %broadcast_multiply_fusion) | copy-start | bytes 3076
  52.0 2.7 copy-start.22
  78.5 29.3 %all-to-all-start.1 = ((bf16[8,2,55296]{2,1,0:T(2,128)(2,1)}), bf16[8,2,55296]{2,1,0:T(2,128)(2,1)}, u32[]{:S(2)}, u32[]{:S(2)}) async-start(bf16[8,2,55296]{2,1,0:T(2,128)(2,1)} %reshape.404), calls=%async_computation.1 | async-start | bytes 3538944 | tf_op jit(solution)/shard_map/all_to_all | solution.py:100
  132.4 11.3 %copy-start.3 = (f32[32,16,8,8]{2,3,1,0:T(8,128)}, f32[32,16,8,8]{2,3,1,0:T(8,128)S(1)}, u32[]{:S(2)}) copy-start(f32[32,16,8,8]{2,3,1,0:T(8,128)S(1)} %get-tuple-element.15) | copy-start | bytes 393220
  132.4 2.0 copy-start.14
  133.4 10.3 %copy-start.19 = (f32[32,16,8]{2,1,0:T(8,128)}, f32[32,16,8]{2,1,0:T(8,128)S(1)}, u32[]{:S(2)}) copy-start(f32[32,16,8]{2,1,0:T(8,128)S(1)} %fusion.56) | copy-start | bytes 49156
  134.4 2.8 copy-start.11
  137.2 2.3 copy-start.13
  139.6 4.1 %copy-start.12 = (bf16[8,32,16,72]{3,2,1,0:T(8,128)(2,1)S(1)}, bf16[8,32,16,72]{3,2,1,0:T(8,128)(2,1)}, u32[]{:S(2)}) copy-start(bf16[8,32,16,72]{3,2,1,0:T(8,128)(2,1)} %reshape.388) | copy-start | bytes 1769476
  151.6 27.5 %all-to-all-start.3 = ((bf16[1,8,32,1152]{3,2,0,1:T(8,128)(2,1)}), bf16[1,8,32,1152]{3,2,0,1:T(8,128)(2,1)}, u32[]{:S(2)}, u32[]{:S(2)}) async-start(bf16[1,8,32,1152]{3,2,0,1:T(8,128)(2,1)} %bitcast.158), calls=%async_computation.3 | async-start | bytes 1179648 | tf_op jit(solution)/shard_map/all_to_all | solution.py:102
  179.1 30.0 %all-to-all-start.2 = ((bf16[1,8,32,3456]{3,2,0,1:T(8,128)(2,1)}), bf16[1,8,32,3456]{3,2,0,1:T(8,128)(2,1)}, u32[]{:S(2)}, u32[]{:S(2)}) async-start(bf16[1,8,32,3456]{3,2,0,1:T(8,128)(2,1)} %add_bitcast_fusion), calls=%async_computation.2 | async-start | bytes 3538944 | tf_op jit(solution)/shard_map/all_to_all | solution.py:108
  185.7 167.4 %all-reduce.9.cloned.1.call-start = ((), (), s32[]{:S(2)}) async-start(), calls=%async_computation.4 | async-start | bytes 10616832
  190.8 18.3 %copy-start.21 = (f32[256]{0:T(256)S(1)}, f32[256]{0:T(256)}, u32[]{:S(2)}) copy-start(f32[256]{0:T(256)} %copy-done.20) | copy-start | bytes 3076
  190.8 18.3 %copy-start.25 = (f32[1152]{0:T(1024)S(1)}, f32[1152]{0:T(1024)}, u32[]{:S(2)}) copy-start(f32[1152]{0:T(1024)} %param.11) | copy-start | bytes 13828
  209.0 6.8 %copy-start.8 = (f32[1,1,256,1152]{3,2,1,0:T(8,128)S(1)}, f32[1,1,256,1152]{3,2,1,0:T(8,128)}, u32[]{:S(2)}) copy-start(f32[1,1,256,1152]{3,2,1,0:T(8,128)} %copy-done.7) | copy-start | bytes 3538948
  209.0 6.8 %copy-start.23 = (f32[256]{0:T(256)S(1)}, f32[256]{0:T(256)}, u32[]{:S(2)}) copy-start(f32[256]{0:T(256)} %copy-done.22) | copy-start | bytes 3076
  215.8 1.5 copy-start.17
  216.3 1.0 copy-start.9
  221.4 4.1 %copy-start.2 = (f32[16,256,256]{1,2,0:T(8,128)S(1)}, f32[16,256,256]{1,2,0:T(8,128)}, u32[]{:S(2)}) copy-start(f32[16,256,256]{1,2,0:T(8,128)} %copy-done.1) | copy-start | bytes 12582916
  225.5 1.2 copy-start.5
  226.7 1.8 copy-start.6
  228.5 2.3 copy-start.16
  228.5 5.4 %slice-start.2 = ((s8[7962624]{0:T(1024)(128)(4,1)}), s8[3768320]{0:T(1024)(128)(4,1)S(1)}, s32[]{:S(2)}) async-start(s8[7962624]{0:T(1024)(128)(4,1)} %bitcast.163), calls=%async_computation.7 | async-start | bytes 7536640
  230.8 3.1 slice-start.3
  230.8 3.1 copy-start.27
  236.7 1.3 copy-start.10
  236.8 1.4 copy-start.18
Sparse Core Ops, SparseCore 0:
  191.5 161.5 all-reduce.8
where the time goes:
time: 368 us; the launch traced here: 362 us
  waiting for transfers between devices  142 us (39%)
  local copies, waits for them, and re-layouts  84.9 us (23%)
  matrix products  65.4 us (18%)
  other arithmetic  27.8 us (8%)
  starting transfers between devices  27.1 us (7%)
  between operations  14.7 us (4%)
    unnamed x2, waiting for transfers between devices  114 us
    unnamed x71, local copies, waits for them, and re-layouts  27.9 us
    dot_general x7, matrix products, project(): return jnp.dot(hidden, weight, preferred_element_type=jnp.float32)  24.4 us
    unnamed x4, other arithmetic  19.1 us
    all_to_all x1, waiting for transfers between devices, per_device(): lax.all_to_all(qkv_grad_pos, 'seq', split_axis=1, concat_axis=2, tiled=True)  18.2 us
    another operation x3, local copies, waits for them, and re-layouts  11.3 us
    dot_general x3, matrix products, temporal_mix(): jnp.einsum('bqphd,bkphd->bphqk', query_part, key_part, precision=lax.Prec...  11.1 us
    all_to_all x1, waiting for transfers between devices, per_device(): lax.all_to_all(qkv, 'seq', split_axis=2, concat_axis=1, tiled=True)  9.94 us
  transfers between devices with their start and end apart: 5, of which 3 were waited for; matrix products, arithmetic and copies ran while one was open for 32% of the time, Pallas kernels for 0%

commit v1 on v0

--- a/solution.py
+++ b/solution.py
@@ -105,7 +105,12 @@
     mixed_grad = out_back(grad_float)[0]
     mixed_grad_pos = lax.all_to_all(mixed_grad, "seq", split_axis=2, concat_axis=1, tiled=True)
     qkv_grad_pos = mix_back(mixed_grad_pos)[0]
-    qkv_grad = lax.all_to_all(qkv_grad_pos, "seq", split_axis=1, concat_axis=2, tiled=True)
+    qkv_grad = jnp.concatenate(
+        lax.all_to_all(
+            jnp.stack(jnp.split(qkv_grad_pos, lax.axis_size("seq"), axis=1)), "seq", 0, 0
+        ),
+        axis=2,
+    )
     stream_grad = grad_float + pre_back(qkv_grad)[0]
     video_grad = spatial_back(stream_grad)[0]
     local_sum = local_sum / math.sqrt(float(token_total))

time: 368 us -> 371 us (level)
  local copies, waits for them, and re-layouts: 84.9 us -> 90.9 us
    unnamed x71 -> x62, local copies, waits for them, and re-layouts: 27.9 us -> 31.9 us
    another operation x3 -> x4, local copies, waits for them, and re-layouts: 11.3 us -> 12 us
where the time goes in v1:
time: 371 us; the launch traced here: 365 us
  waiting for transfers between devices  142 us (38%)
  local copies, waits for them, and re-layouts  90.9 us (25%)
  matrix products  64.3 us (17%)
  starting transfers between devices  26.7 us (7%)
  other arithmetic  26.4 us (7%)
  between operations  14.6 us (4%)
    unnamed x2, waiting for transfers between devices  114 us
    unnamed x62, local copies, waits for them, and re-layouts  31.9 us
    dot_general x7, matrix products, project(): return jnp.dot(hidden, weight, preferred_element_type=jnp.float32)  24.4 us
    unnamed x4, other arithmetic  19 us
    all_to_all x1, waiting for transfers between devices, per_device(): lax.all_to_all(jnp.stack(jnp.split(qkv_grad_pos, lax.axis_size('seq'), ax...  18.3 us
    another operation x3, local copies, waits for them, and re-layouts  11.2 us
    dot_general x3, matrix products, temporal_mix(): jnp.einsum('bqphd,bkphd->bphqk', query_part, key_part, precision=lax.Prec...  11.1 us
    all_to_all x1, waiting for transfers between devices, per_device(): lax.all_to_all(qkv, 'seq', split_axis=2, concat_axis=1, tiled=True)  9.96 us
  transfers between devices with their start and end apart: 5, of which 3 were waited for; matrix products, arithmetic and copies ran while one was open for 32% of the time, Pallas kernels for 0%

profile of v1, /device:TPU:1, one launch (start us, length us, event | category | flops | bytes accessed | tf_op | source)
XLA Modules:
  0.0 365.0 jit_solution(17450298150345353612)
XLA Ops:
  7.2 3.1 fusion.7
  12.7 6.0 %reduce.23 = bf16[256,1152]{1,0:T(8,128)(2,1)} reduce(bf16[256,1,1,1152]{3,2,1,0:T(2,128)(2,1)} %bitcast.183, bf16[]{:T(256)} %broadcast.212), dimensions={1,2}, to_apply=%bitcast.175.reduce_sub_computation | reduce | bytes 1179650
  18.7 2.6 reshape.404
  21.3 7.7 %all-to-all-start = ((bf16[8,2,18432]{2,1,0:T(2,128)(2,1)}), bf16[8,2,18432]{2,1,0:T(2,128)(2,1)}, u32[]{:S(2)}, u32[]{:S(2)}) async-start(bf16[8,2,18432]{2,1,0:T(2,128)(2,1)} %reshape.404), calls=%async_computation | async-start | bytes 1179648 | tf_op jit(solution)/shard_map/all_to_all | solution.py:106
  29.5 5.9 %fusion = bf16[1,1,256,3456]{3,2,1,0:T(8,128)(2,1)S(1)} fusion(bf16[1152,3456]{1,0:T(8,128)(2,1)} %param.12, bf16[1,1,256,1152]{3,2,1,0:T(8,128)(2,1)S(1)} %copy-done.3, f32[1152]{0:T(1024)S(1)} %copy-done.19, f32[256]{0:T(256)S(1)} %fusion.65, f32[256]{0:T(256)S(1)} %broadcast_multiply_fusion.1), kind=kOutput, calls=%fused_computation.3 | convolution fusion | flops 2040791040 | bytes 10328576 | tf_op jit(solution)/shard_map/jvp()/dot_general | solution.py:19
  36.7 2.1 copy.72
  38.9 2.1 copy.71
  41.0 2.1 copy.70
  43.1 2.0 multiply_reduce_fusion.1
  47.3 2.4 convolution_convert_fusion.13
  51.9 2.7 fusion.1
  54.6 5.0 %copy.129 = bf16[1,1,256,3456]{3,1,0,2:T(2,128)(2,1)} copy(bf16[1,1,256,3456]{3,2,1,0:T(8,128)(2,1)S(1)} %fusion.1) | data formatting | bytes 3538944 | tf_op jit(solution)/shard_map/jvp()/convert_element_type | solution.py:95
  59.6 13.0 %reduce.22 = bf16[256,3456]{1,0:T(8,128)(2,1)} reduce(bf16[256,1,1,3456]{3,2,1,0:T(2,128)(2,1)} %bitcast.176, bf16[]{:T(256)} %broadcast.212), dimensions={1,2}, to_apply=%bitcast.174.reduce_sub_computation | reduce | bytes 3538946
  72.6 5.7 %reshape.402 = bf16[8,2,55296]{2,1,0:T(2,128)(2,1)} reshape(bf16[256,3456]{1,0:T(8,128)(2,1)} %reduce.22) | data formatting | bytes 3538944
  78.3 6.6 %all-to-all-start.1 = ((bf16[8,2,55296]{2,1,0:T(2,128)(2,1)}), bf16[8,2,55296]{2,1,0:T(2,128)(2,1)}, u32[]{:S(2)}, u32[]{:S(2)}) async-start(bf16[8,2,55296]{2,1,0:T(2,128)(2,1)} %reshape.402), calls=%async_computation.1 | async-start | bytes 3538944 | tf_op jit(solution)/shard_map/all_to_all | solution.py:100
  84.9 3.5 reshape.405
  88.5 5.5 %bitcast_reduce_fusion = bf16[256,1152]{1,0:T(8,128)(2,1)} fusion(bf16[256,1,1,1152]{3,2,1,0:T(2,128)(2,1)} %reshape.405), kind=kLoop, calls=%fused_computation.131 | loop fusion | bytes 1179648 | tf_op jit(solution)/shard_map/all_to_all | solution.py:106
  94.0 3.7 %reshape.379 = bf16[1,8,32,16,72]{4,3,2,1,0:T(8,128)(2,1)} reshape(bf16[256,1152]{1,0:T(8,128)(2,1)} %bitcast_reduce_fusion) | data formatting | bytes 1179648 | tf_op jit(solution)/shard_map/transpose(jvp())/reshape | solution.py:54
  97.7 10.0 %all-to-all-done.1 = bf16[8,2,55296]{2,1,0:T(2,128)(2,1)} async-done(((bf16[8,2,55296]{2,1,0:T(2,128)(2,1)}), bf16[8,2,55296]{2,1,0:T(2,128)(2,1)}, u32[]{:S(2)}, u32[]{:S(2)}) %all-to-all-start.1) | async-done | bytes 1769504 | tf_op jit(solution)/shard_map/all_to_all | solution.py:100
  107.6 6.5 %reshape.403 = bf16[256,1,1,3456]{3,2,1,0:T(2,128)(2,1)} reshape(bf16[8,2,55296]{2,1,0:T(2,128)(2,1)} %all-to-all-done.1) | data formatting | bytes 3538944
  114.2 2.2 copy.98
  117.7 3.7 %reshape.386 = bf16[8,32,16,72]{3,2,1,0:T(8,128)(2,1)} reshape(bf16[1,8,32,1152]{3,2,1,0:T(8,128)(2,1)} %get-tuple-element.4) | data formatting | bytes 1179648 | tf_op jit(solution)/shard_map/reshape.55
  121.4 3.7 %reshape.389 = bf16[8,32,16,72]{3,2,1,0:T(8,128)(2,1)} reshape(bf16[1,8,32,1152]{3,2,1,0:T(8,128)(2,1)} %get-tuple-element.5) | data formatting | bytes 1179648 | tf_op jit(solution)/shard_map/reshape.64
  125.1 3.9 %reshape.387 = bf16[8,32,16,72]{3,2,1,0:T(8,128)(2,1)} reshape(bf16[1,8,32,1152]{3,2,1,0:T(8,128)(2,1)} %get-tuple-element.6) | data formatting | bytes 1179648 | tf_op jit(solution)/shard_map/reshape.56
  128.9 3.2 multiply_reduce_fusion.3
  133.4 2.8 fusion.22
  136.2 3.6 fusion.19
  139.8 2.3 multiply_reduce_fusion.2
  142.1 4.1 %fusion.21 = bf16[1,8,32,16,72]{4,1,3,2,0:T(8,128)(2,1)} fusion(bf16[8,32,16,72]{3,2,1,0:T(8,128)(2,1)S(1)} %copy-done.12, f32[32,16,8,8]{2,3,1,0:T(8,128)S(1)} %get-tuple-element.17, f32[32,16,8]{2,1,0:T(8,128)S(1)} %neg.20, f32[32,16,8]{2,1,0:T(8,128)S(1)} %fusion.64, f32[32,16,8]{2,1,0:T(8,128)S(1)} %get-tuple-element.14, ...), kind=kOutput, calls=%fused_computation.47 | convolution fusion | flops 28803072 | bytes 1490944 | tf_op jit(solution)/shard_map/transpose(jvp(bqphd,bkphd->bphqk))/dot_general | solution.py:49
  146.2 3.8 %fusion.20 = bf16[1,8,32,16,72]{4,1,3,2,0:T(8,128)(2,1)} fusion(bf16[8,32,16,72]{3,2,1,0:T(8,128)(2,1)S(1)} %copy-done.11, f32[32,16,8,8]{2,3,1,0:T(8,128)S(1)} %get-tuple-element.17, f32[32,16,8]{2,1,0:T(8,128)S(1)} %neg.20, f32[32,16,8]{2,1,0:T(8,128)S(1)} %fusion.64, f32[32,16,8]{2,1,0:T(8,128)S(1)} %get-tuple-element.14, ...), kind=kOutput, calls=%fused_computation.46 | convolution fusion | flops 28803072 | bytes 1490944 | tf_op jit(solution)/shard_map/transpose(jvp(bqphd,bkphd->bphqk))/dot_general | solution.py:49
  151.2 2.9 convert_element_type.198
  154.1 5.2 %all-to-all-start.3 = ((bf16[1,8,32,1152]{3,2,0,1:T(8,128)(2,1)}), bf16[1,8,32,1152]{3,2,0,1:T(8,128)(2,1)}, u32[]{:S(2)}, u32[]{:S(2)}) async-start(bf16[1,8,32,1152]{3,2,0,1:T(8,128)(2,1)} %bitcast.188), calls=%async_computation.3 | async-start | bytes 1179648 | tf_op jit(solution)/shard_map/all_to_all | solution.py:102
  159.3 2.4 copy.77
  161.7 2.9 reshape.388
  164.6 2.3 copy.80
  166.9 2.9 reshape.390
  169.8 2.3 copy.83
  172.2 2.9 reshape.391
  182.3 6.6 %all-to-all-start.2 = ((bf16[8,1,1,32,3456]{4,3,2,1,0:T(8,128)(2,1)}), bf16[8,1,1,32,3456]{4,3,2,1,0:T(8,128)(2,1)}, u32[]{:S(2)}, u32[]{:S(2)}) async-start(bf16[8,1,1,32,3456]{4,3,2,1,0:T(8,128)(2,1)} %fusion.56), calls=%async_computation.2 | async-start | bytes 3538944 | tf_op jit(solution)/shard_map/all_to_all | solution.py:109
  189.5 4.5 %convolution_multiply_fusion = f32[1152,1152]{1,0:T(8,128)} fusion(bf16[256,1152]{1,0:T(8,128)(2,1)} %bitcast.54, bf16[1,1,256,1152]{3,2,1,0:T(8,128)(2,1)} %param.9), kind=kOutput, calls=%fused_computation | convolution fusion | flops 680804352 | bytes 6488064 | tf_op jit(solution)/shard_map/dot_general | solution.py:65
  194.0 18.3 %all-to-all-done.2 = bf16[8,1,1,32,3456]{4,3,2,1,0:T(8,128)(2,1)} async-done(((bf16[8,1,1,32,3456]{4,3,2,1,0:T(8,128)(2,1)}), bf16[8,1,1,32,3456]{4,3,2,1,0:T(8,128)(2,1)}, u32[]{:S(2)}, u32[]{:S(2)}) %all-to-all-start.2) | async-done | bytes 1769504 | tf_op jit(solution)/shard_map/all_to_all | solution.py:109
  212.3 6.8 %fusion.28 = (f32[256]{0:T(256)S(1)}, f32[256,1152]{1,0:T(8,128)S(1)}) fusion(f32[1,1,256,1152]{3,2,1,0:T(8,128)} %copy-done.6, f32[256]{0:T(256)S(1)} %broadcast_multiply_fusion, f32[1152]{0:T(1024)S(1)} %copy-done.18, bf16[256,3456]{1,0:T(8,128)(2,1)} %bitcast.30, bf16[1152,3456]{1,0:T(8,128)(2,1)} %param.14), kind=kOutput, calls=%fused_computation.59 | convolution fusion | flops 2040200960 | bytes 12098048 | tf_op jit(solution)/shard_map/transpose(jvp())/dot_general | solution.py:19
  222.5 2.2 copy.84
  224.6 4.1 %multiply_reduce_fusion = (f32[16,256]{1,0:T(8,128)S(1)}, f32[16,256,256]{1,2,0:T(8,128)S(1)}) fusion(f32[16,256]{1,0:T(8,128)S(1)} %multiply_divide_fusion.1, f32[16,256]{1,0:T(8,128)S(1)} %get-tuple-element.10, f32[16,256,256]{1,2,0:T(8,128)} %copy-done.1, bf16[16,72,256]{2,1,0:T(8,128)(2,1)} %bitcast.186, bf16[256,16,72]{0,2,1:T(8,128)(2,1)} %bitcast.184), kind=kOutput, calls=%fused_computation.6 | convolution fusion | flops 156233728 | bytes 9617408 | tf_op jit(solution)/shard_map/transpose(jvp(bfhqk,bfkhd->bfqhd))/dot_general | solution.py:38
  231.8 2.3 convolution_convert_fusion.11
  234.1 3.1 convolution_convert_fusion.12
  237.2 2.8 fusion.26
  242.8 113.7 %all-reduce.9.cloned.1.call-done = f32[1152,1152]{1,0:T(8,128)} async-done(((f32[1152,1152]{1,0:T(8,128)}), f32[1152,1152]{1,0:T(8,128)}) %all-reduce.9.cloned.1.call-update) | async-done | bytes 5308432
  (93 shorter events, 30.4 us)
Async XLA Ops:
  7.2 42.5 %copy-start = (bf16[1152,1152]{1,0:T(8,128)(2,1)S(1)}, bf16[1152,1152]{1,0:T(8,128)(2,1)}, u32[]{:S(2)}) copy-start(bf16[1152,1152]{1,0:T(8,128)(2,1)} %param.13) | copy-start | bytes 7962628
  12.2 16.8 %copy-start.3 = (bf16[1,1,256,1152]{3,2,1,0:T(8,128)(2,1)S(1)}, bf16[1,1,256,1152]{3,2,1,0:T(8,128)(2,1)}, u32[]{:S(2)}) copy-start(bf16[1,1,256,1152]{3,2,1,0:T(8,128)(2,1)} %param.8) | copy-start | bytes 1769476
  18.7 10.8 %copy-start.19 = (f32[1152]{0:T(1024)S(1)}, f32[1152]{0:T(1024)}, u32[]{:S(2)}) copy-start(f32[1152]{0:T(1024)} %param.10) | copy-start | bytes 13828
  21.3 57.0 %all-to-all-start = ((bf16[8,2,18432]{2,1,0:T(2,128)(2,1)}), bf16[8,2,18432]{2,1,0:T(2,128)(2,1)}, u32[]{:S(2)}, u32[]{:S(2)}) async-start(bf16[8,2,18432]{2,1,0:T(2,128)(2,1)} %reshape.404), calls=%async_computation | async-start | bytes 1179648 | tf_op jit(solution)/shard_map/all_to_all | solution.py:106
  45.1 2.1 copy-start.1
  45.1 2.1 copy-start.14
  45.1 6.7 %slice-start = ((s8[7962624]{0:T(1024)(128)(4,1)}), s8[4194304]{0:T(1024)(128)(4,1)S(1)}, s32[]{:S(2)}) async-start(s8[7962624]{0:T(1024)(128)(4,1)} %bitcast.191), calls=%async_computation.5 | async-start | bytes 8388608
  47.3 4.6 %slice-start.1 = ((s8[7962624]{0:T(1024)(128)(4,1)}), s8[3768320]{0:T(1024)(128)(4,1)S(1)}, s32[]{:S(2)}) async-start(s8[7962624]{0:T(1024)(128)(4,1)} %bitcast.191), calls=%async_computation.6 | async-start | bytes 7536640
  49.7 2.2 copy-start.18
  50.8 1.0 copy-start.6
  78.3 29.4 %all-to-all-start.1 = ((bf16[8,2,55296]{2,1,0:T(2,128)(2,1)}), bf16[8,2,55296]{2,1,0:T(2,128)(2,1)}, u32[]{:S(2)}, u32[]{:S(2)}) async-start(bf16[8,2,55296]{2,1,0:T(2,128)(2,1)} %reshape.402), calls=%async_computation.1 | async-start | bytes 3538944 | tf_op jit(solution)/shard_map/all_to_all | solution.py:100
  132.1 1.2 copy-start.13
  133.4 2.8 copy-start.10
  139.8 2.3 copy-start.12
  142.1 4.1 %copy-start.11 = (bf16[8,32,16,72]{3,2,1,0:T(8,128)(2,1)S(1)}, bf16[8,32,16,72]{3,2,1,0:T(8,128)(2,1)}, u32[]{:S(2)}) copy-start(bf16[8,32,16,72]{3,2,1,0:T(8,128)(2,1)} %reshape.386) | copy-start | bytes 1769476
  154.1 28.2 %all-to-all-start.3 = ((bf16[1,8,32,1152]{3,2,0,1:T(8,128)(2,1)}), bf16[1,8,32,1152]{3,2,0,1:T(8,128)(2,1)}, u32[]{:S(2)}, u32[]{:S(2)}) async-start(bf16[1,8,32,1152]{3,2,0,1:T(8,128)(2,1)} %bitcast.188), calls=%async_computation.3 | async-start | bytes 1179648 | tf_op jit(solution)/shard_map/all_to_all | solution.py:102
  182.3 30.0 %all-to-all-start.2 = ((bf16[8,1,1,32,3456]{4,3,2,1,0:T(8,128)(2,1)}), bf16[8,1,1,32,3456]{4,3,2,1,0:T(8,128)(2,1)}, u32[]{:S(2)}, u32[]{:S(2)}) async-start(bf16[8,1,1,32,3456]{4,3,2,1,0:T(8,128)(2,1)} %fusion.56), calls=%async_computation.2 | async-start | bytes 3538944 | tf_op jit(solution)/shard_map/all_to_all | solution.py:109
  189.0 167.4 %all-reduce.9.cloned.1.call-start = ((), (), s32[]{:S(2)}) async-start(), calls=%async_computation.4 | async-start | bytes 10616832
  212.3 6.8 %copy-start.7 = (f32[1,1,256,1152]{3,2,1,0:T(8,128)S(1)}, f32[1,1,256,1152]{3,2,1,0:T(8,128)}, u32[]{:S(2)}) copy-start(f32[1,1,256,1152]{3,2,1,0:T(8,128)} %copy-done.6) | copy-start | bytes 3538948
  219.1 1.5 copy-start.16
  219.5 1.0 copy-start.8
  224.6 4.1 %copy-start.2 = (f32[16,256,256]{1,2,0:T(8,128)S(1)}, f32[16,256,256]{1,2,0:T(8,128)}, u32[]{:S(2)}) copy-start(f32[16,256,256]{1,2,0:T(8,128)} %copy-done.1) | copy-start | bytes 12582916
  228.8 1.2 copy-start.4
  230.0 1.8 copy-start.5
  231.8 2.3 copy-start.15
  231.8 5.4 %slice-start.2 = ((s8[7962624]{0:T(1024)(128)(4,1)}), s8[3768320]{0:T(1024)(128)(4,1)S(1)}, s32[]{:S(2)}) async-start(s8[7962624]{0:T(1024)(128)(4,1)} %bitcast.193), calls=%async_computation.7 | async-start | bytes 7536640
  234.1 3.1 slice-start.3
  240.0 1.3 copy-start.9
  240.0 1.4 copy-start.17
Sparse Core Ops, SparseCore 0:
  194.7 161.6 all-reduce.8
